TPU v7x, 32 devices: a whole 2x2x4 slice. The times are simulated.
32 devices in a mesh: seq: 8 (over y, x, core), grp: 4 (over z).
Axes of the slice: x: 2, y: 2, z: 4, core: 2. Of those that a mesh axis runs over, the one named last changes fastest.
Arguments:
- queries: bfloat16 [8192, 4096], P(('grp', 'seq')), parts along dimension 0, may hold values from -64 to 64
- keys: bfloat16 [8192, 1024], P(('grp', 'seq')), parts along dimension 0, may hold values from -64 to 64
- values: bfloat16 [8192, 1024], P(('grp', 'seq')), parts along dimension 0, may hold values from -6 to 6
- doc_lengths: int32 [24], P('grp'), parts along dimension 0, may hold values from 1 to 8, 16 in all
Outputs:
- attended: bfloat16 [8192, 4096], P(('grp', 'seq')), parts along dimension 0
There are 4 independent parts, one for each index of `grp`. A program takes and returns all parts, laid end to end along the dimension named above; each array names one. Nothing has to cross between parts.
Inputs may be any that keep to these rules, and one draw needn't show every extreme that they name: `doc_lengths`: lengths of the documents in units of 128 tokens, summing to 16.
All inputs are finite; a program needn't handle non-finite values.
Results may differ from a plain program's by a relative error of at most 0.004.
Values may be sent and summed in bfloat16 or wider, within the bound.
No kernel may reach another device: no remote copies, remote signals or barrier semaphores. Data moves between devices by JAX's collectives and lax.ppermute only.
A program may use at most 128 MiB of HBM per device.

v0:
```python
import jax
import jax.numpy as jnp
from jax import lax
from jax.sharding import PartitionSpec as P

HEAD_DIM = 128
DOC_UNIT = 128
lowest = -1e30


def doc_starts(doc_lengths):
    lengths = doc_lengths * DOC_UNIT
    return jnp.cumsum(lengths) - lengths


def doc_ids(positions, starts):
    return jnp.sum((positions[:, None] >= starts[None, :]).astype(jnp.int32), axis=1)


def pick_width(total_rows, unit_rows):
    shard_count = total_rows // unit_rows
    most_factor = max(1, 1024 // unit_rows)
    chosen = 1
    for factor in range(1, most_factor + 1):
        if shard_count % factor == 0:
            chosen = factor
    return unit_rows * chosen


def fresh_state(kv_count, group_size, query_rows, head_dim):
    maxima = jnp.full((kv_count, group_size, query_rows), lowest, jnp.float32)
    totals = jnp.zeros((kv_count, group_size, query_rows), jnp.float32)
    accumulated = jnp.zeros((kv_count, group_size, query_rows, head_dim), jnp.float32)
    return (maxima, totals, accumulated)


def update(running, query_rows, query_pos, query_doc, key_part, value_part, key_pos, key_doc):
    scale = query_rows.shape[-1] ** (-0.5)
    needed = (
        (key_pos[0] <= query_pos[-1])
        & (key_doc[-1] >= query_doc[0])
        & (key_doc[0] <= query_doc[-1])
    )

    def compute(current):
        maxima, totals, accumulated = current
        allowed = (key_pos[None, :] <= query_pos[:, None]) & (
            key_doc[None, :] == query_doc[:, None]
        )
        scores = (
            jnp.einsum("qhgd,khd->hgqk", query_rows, key_part, preferred_element_type=jnp.float32)
            * scale
        )
        scores = jnp.where(allowed[None, None], scores, lowest)
        new_max = jnp.maximum(maxima, jnp.max(scores, axis=-1))
        weights = jnp.where(allowed[None, None], jnp.exp(scores - new_max[..., None]), 0.0)
        rescale = jnp.exp(maxima - new_max)
        totals = totals * rescale + jnp.sum(weights, axis=-1)
        mixed = jnp.einsum(
            "hgqk,khd->hgqd",
            weights.astype(jnp.bfloat16),
            value_part,
            preferred_element_type=jnp.float32,
        )
        accumulated = accumulated * rescale[..., None] + mixed
        return (new_max, totals, accumulated)

    def unchanged(current):
        return current

    return lax.cond(needed, compute, unchanged, running)


def sweep_keys(
    running, query_rows, query_pos, query_doc, key_rows, value_rows, key_start, all_docs, unit_rows
):
    total_rows = key_rows.shape[0]
    block_rows = pick_width(total_rows, unit_rows)
    turns = total_rows // block_rows

    def advance(number, current):
        offset = number * block_rows
        key_part = lax.dynamic_slice_in_dim(key_rows, offset, block_rows, 0)
        value_part = lax.dynamic_slice_in_dim(value_rows, offset, block_rows, 0)
        first_key = (key_start + offset).astype(jnp.int32)
        key_pos = first_key + jnp.arange(block_rows, dtype=jnp.int32)
        key_doc = lax.dynamic_slice_in_dim(all_docs, first_key, block_rows, 0)
        return update(
            current, query_rows, query_pos, query_doc, key_part, value_part, key_pos, key_doc
        )

    return lax.fori_loop(0, turns, advance, running)


def finish(running):
    maxima, totals, accumulated = running
    result = accumulated / totals[..., None]
    kv_count, group_size, query_rows, head_dim = result.shape
    return (
        result.transpose(2, 0, 1, 3)
        .reshape(query_rows, kv_count * group_size * head_dim)
        .astype(jnp.bfloat16)
    )


def on_device(queries, keys, values, doc_lengths):
    row_count = queries.shape[0]
    head_dim = HEAD_DIM
    kv_total = keys.shape[1] // head_dim
    heads_total = queries.shape[1] // head_dim
    group_size = heads_total // kv_total
    seq_count = lax.axis_size("seq")
    starts = doc_starts(doc_lengths)
    every_pos = jnp.arange(row_count * seq_count, dtype=jnp.int32)
    all_docs = doc_ids(every_pos, starts)
    heads_dev = heads_total // seq_count
    kv_dev = max(1, heads_dev // group_size)
    repeat_count = max(1, group_size // heads_dev)
    sub_group = heads_dev // kv_dev
    key_send = jnp.repeat(
        keys.reshape(row_count, kv_total, head_dim), repeat_count, axis=1
    ).reshape(row_count, seq_count * kv_dev * head_dim)
    value_send = jnp.repeat(
        values.reshape(row_count, kv_total, head_dim), repeat_count, axis=1
    ).reshape(row_count, seq_count * kv_dev * head_dim)
    all_queries, all_keys, all_values = (
        lax.all_to_all(queries, "seq", split_axis=1, concat_axis=0, tiled=True),
        lax.all_to_all(key_send, "seq", split_axis=1, concat_axis=0, tiled=True),
        lax.all_to_all(value_send, "seq", split_axis=1, concat_axis=0, tiled=True),
    )
    total_rows = all_queries.shape[0]
    all_keys = all_keys.reshape(total_rows, kv_dev, head_dim)
    all_values = all_values.reshape(total_rows, kv_dev, head_dim)
    block_rows = pick_width(total_rows, row_count)
    block_count = total_rows // block_rows
    query_blocks = all_queries.reshape(block_count, block_rows, kv_dev, sub_group, head_dim)

    def attend_block(inputs):
        query_part, number = inputs
        first_query = number * block_rows
        query_pos = first_query + jnp.arange(block_rows, dtype=jnp.int32)
        query_doc = lax.dynamic_slice_in_dim(all_docs, first_query, block_rows, 0)
        running = sweep_keys(
            fresh_state(kv_dev, sub_group, block_rows, head_dim),
            query_part,
            query_pos,
            query_doc,
            all_keys,
            all_values,
            0,
            all_docs,
            row_count,
        )
        return finish(running)

    outputs = lax.map(attend_block, (query_blocks, jnp.arange(block_count, dtype=jnp.int32)))
    outputs = outputs.reshape(total_rows, heads_dev * head_dim)
    return lax.all_to_all(outputs, "seq", split_axis=0, concat_axis=1, tiled=True)


def solution(mesh):
    placed = (P(("grp", "seq"), None), P(("grp", "seq"), None), P(("grp", "seq"), None), P("grp"))
    return jax.shard_map(
        on_device, mesh=mesh, in_specs=placed, out_specs=P(("grp", "seq"), None), check_vma=False
    )
```

profile of v0, /device:TPU:0, one launch (start us, length us, event | category | flops | bytes accessed | tf_op | source)
XLA Modules:
  0.0 189.1 jit_solution(11757262031421590637)
XLA Ops:
  0.0 1.0 copy-done
  1.0 0.9 copy_bitcast_fusion.3
  1.9 5.2 %all-to-all-start.1 = ((bf16[256,8,128]{2,0,1:T(8,128)(2,1)}), bf16[256,8,128]{2,0,1:T(8,128)(2,1)S(1)}, u32[]{:S(2)}, u32[]{:S(2)}) async-start(bf16[256,8,128]{2,0,1:T(8,128)(2,1)} %copy_bitcast_fusion.3), calls=%async_computation.1 | async-start | bytes 1048576 | tf_op jit(solution)/shard_map/all_to_all | solution.py:128
  7.1 3.1 %copy.49 = bf16[32,8,8,512]{3,2,0,1:T(8,128)(2,1)} copy(bf16[32,8,8,512]{3,2,1,0:T(8,128)(2,1)} %bitcast.104) | data formatting | bytes 4194304 | tf_op jit(solution)/shard_map/all_to_all | solution.py:127
  10.3 6.6 %all-to-all-done.1 = bf16[256,8,128]{2,0,1:T(8,128)(2,1)S(1)} async-done(((bf16[256,8,128]{2,0,1:T(8,128)(2,1)}), bf16[256,8,128]{2,0,1:T(8,128)(2,1)S(1)}, u32[]{:S(2)}, u32[]{:S(2)}) %all-to-all-start.1) | async-done | bytes 524320 | tf_op jit(solution)/shard_map/all_to_all | solution.py:128
  16.8 3.6 %all-to-all-start = ((bf16[256,8,512]{2,0,1:T(8,128)(2,1)}), bf16[256,8,512]{2,0,1:T(8,128)(2,1)S(1)}, u32[]{:S(2)}, u32[]{:S(2)}) async-start(bf16[256,8,512]{2,0,1:T(8,128)(2,1)} %bitcast.102), calls=%async_computation | async-start | bytes 4194304 | tf_op jit(solution)/shard_map/all_to_all | solution.py:127
  20.5 1.9 %copy_bitcast_fusion.2 = bf16[256,8,128]{2,0,1:T(8,128)(2,1)} fusion(bf16[256,1024]{1,0:T(8,128)(2,1)} %param.12), kind=kLoop, calls=%fused_computation.33 | loop fusion | bytes 1048576 | tf_op jit(solution)/shard_map/all_to_all | solution.py:129
  22.4 24.6 %all-to-all-done = bf16[256,8,512]{2,0,1:T(8,128)(2,1)S(1)} async-done(((bf16[256,8,512]{2,0,1:T(8,128)(2,1)}), bf16[256,8,512]{2,0,1:T(8,128)(2,1)S(1)}, u32[]{:S(2)}, u32[]{:S(2)}) %all-to-all-start) | async-done | bytes 2097184 | tf_op jit(solution)/shard_map/all_to_all | solution.py:127
  47.0 4.1 %all-to-all-start.2 = ((bf16[256,8,128]{2,0,1:T(8,128)(2,1)}), bf16[256,8,128]{2,0,1:T(8,128)(2,1)}, u32[]{:S(2)}, u32[]{:S(2)}) async-start(bf16[256,8,128]{2,0,1:T(8,128)(2,1)} %copy_bitcast_fusion.2), calls=%async_computation.2 | async-start | bytes 1048576 | tf_op jit(solution)/shard_map/all_to_all | solution.py:129
  51.5 2.1 %reshape.181 = bf16[2,1024,1,4,128]{4,3,1,0,2:T(4,128)(2,1)} reshape(bf16[8,256,512]{2,1,0:T(8,128)(2,1)S(1)} %bitcast.101) | data formatting | bytes 4194304 | tf_op jit(solution)/shard_map/reshape | solution.py:136
  53.6 7.3 %all-to-all-done.2 = bf16[256,8,128]{2,0,1:T(8,128)(2,1)} async-done(((bf16[256,8,128]{2,0,1:T(8,128)(2,1)}), bf16[256,8,128]{2,0,1:T(8,128)(2,1)}, u32[]{:S(2)}, u32[]{:S(2)}) %all-to-all-start.2) | async-done | bytes 524320 | tf_op jit(solution)/shard_map/all_to_all | solution.py:129
  61.5 91.1 %while.28 = (s32[]{:T(128)}, bf16[2,1024,512]{2,1,0:T(8,128)(2,1)}, s32[2]{0:T(128)}, s32[2048]{0:T(1024)S(1)}, bf16[2,1024,1,4,128]{4,3,1,0,2:T(4,128)(2,1)}, /...) while((s32[]{:T(128)}, bf16[2,1024,512]{2,1,0:T(8,128)(2,1)}, ...), condition=%wide.region_9.10_spmd, body=%wide.region_2.9_spmd.sunk | while | flops 2207266816 | bytes 93153088 | solution.py:156
  61.5 1.3 dynamic_slice.58
  63.5 1.6 constant_dynamic-slice_fusion.2
  65.2 1.4 broadcast.86
  66.7 27.9 %while.29 = (s32[]{:T(128)}, f32[1,4,1024]{2,1,0:T(4,128)S(1)}, f32[1,4,1024]{2,1,0:T(4,128)S(1)}, f32[1,4,1024,128]{3,2,1,0:T(8,128)}, s32[1024]{0:T(1024)S(1)}...) while((s32[]{:T(128)}, f32[1,4,1024]{2,1,0:T(4,128)S(1)}, ...), condition=%wide.region_8.8_spmd, body=%wide.region_3.7_spmd.sunk | while | flops 2206217216 | bytes 77362136 | solution.py:92
  72.5 16.3 %conditional.2 = ((f32[1,4,1024]{2,1,0:T(4,128)S(1)}, f32[1,4,1024]{2,1,0:T(4,128)S(1)}, f32[1,4,1024,128]{3,2,1,0:T(8,128)})) conditional(s32[]{:T(128)} %bitcast.95, (f32[1,4,1024]{2,1,0:T(4,128)S(1)}, f32[1,4,1024]{2,1,0:T(4,128)S(1)}, f32[1,4,1024,128]{3,2,1,0:T(8,128)}) %tuple.69, (s32[1024]{0:T(1024)S(1)}, s32[1024]{0:T(1024)S(1)}, ...), branch_computations={%region_4.3_spmd, %region_5.6_spmd} | conditional | flops 2206216192 | bytes 77349464 | solution.py:71
  72.5 1.2 compare_and_fusion
  73.7 3.1 %fusion = (f32[4,1024]{1,0:T(4,128)S(1)}, f32[1024,1024,4]{1,0,2:T(8,128)S(1)}) fusion(pred[1024,1024]{0,1:T(8,128)(4,1)S(1)} %compare_and_fusion, bf16[1024,1,4,128]{3,0,2,1:T(8,128)(2,1)S(1)} %get-tuple-element.284, bf16[2048,1,128]{2,0,1:T(8,128)(2,1)S(1)} %get-tuple-element.282, s32[]{:T(128)} %get-tuple-element.283), kind=kOutput, calls=%fused_computation.2 | convolution fusion | flops 1086320640 | bytes 19152900 | tf_op jit(solution)/shard_map/while/body/eval_jaxpr/while/body/eval_jaxpr/cond/branch_1_fun/qhgd,khd->hgqk/dot_general | solution.py:51
  76.9 4.2 %fusion.2 = f32[4,1024]{1,0:T(4,128)S(1)} fusion(f32[1024,1024,4]{1,0,2:T(8,128)S(1)} %get-tuple-element.379, f32[4,1024]{1,0:T(4,128)S(1)} %bitcast.97, pred[1024,1024]{0,1:T(8,128)(4,1)S(1)} %compare_and_fusion), kind=kLoop, calls=%fused_computation.4 | loop fusion | flops 20967424 | bytes 17858560 | tf_op jit(solution)/shard_map/while/body/eval_jaxpr/while/body/eval_jaxpr/cond/branch_1_fun/reduce_sum | solution.py:58
  81.1 6.4 %bitcast_add_fusion = f32[1,4,1024,128]{3,2,1,0:T(8,128)S(1)} fusion(f32[1,4,1024,128]{3,2,1,0:T(8,128)S(1)} %copy-done.1, f32[1024,1024,4]{1,0,2:T(8,128)S(1)} %get-tuple-element.379, f32[4,1024]{1,0:T(4,128)S(1)} %bitcast.98, pred[1024,1024]{0,1:T(8,128)(4,1)S(1)} %compare_and_fusion, f32[4,1024]{1,0:T(4,128)S(1)} %get-tuple-element.376, ...), kind=kOutput, calls=%fused_computation.9 | convolution fusion | flops 1095761920 | bytes 22315520 | tf_op jit(solution)/shard_map/while/body/eval_jaxpr/while/body/eval_jaxpr/cond/branch_1_fun/hgqk,khd->hgqd/dot_general | solution.py:59
  87.5 1.3 copy-done.2
  88.8 0.7 fusion.29
  94.6 2.0 %fusion.28 = bf16[1024,1,4,128]{3,0,2,1:T(8,128)(2,1)S(1)} fusion(f32[1,4,1024,128]{3,2,1,0:T(8,128)} %get-tuple-element.510, f32[4,1024]{1,0:T(4,128)S(1)} %bitcast.100), kind=kLoop, calls=%fused_computation.28.clone.1 | loop fusion | flops 1048576 | bytes 3162112 | tf_op jit(solution)/shard_map/while/body/eval_jaxpr/convert_element_type | solution.py:102
  96.6 0.8 copy.53
  97.8 1.0 constant_dynamic-update-slice_fusion.2
  98.9 1.3 dynamic_slice.58
  100.9 1.6 constant_dynamic-slice_fusion.2
  102.7 1.4 broadcast.86
  104.1 44.2 %while.29 = (s32[]{:T(128)}, f32[1,4,1024]{2,1,0:T(4,128)S(1)}, f32[1,4,1024]{2,1,0:T(4,128)S(1)}, f32[1,4,1024,128]{3,2,1,0:T(8,128)}, s32[1024]{0:T(1024)S(1)}...) while((s32[]{:T(128)}, f32[1,4,1024]{2,1,0:T(4,128)S(1)}, ...), condition=%wide.region_8.8_spmd, body=%wide.region_3.7_spmd.sunk | while | flops 2206217216 | bytes 77362136 | solution.py:92
  109.9 16.3 %conditional.2 = ((f32[1,4,1024]{2,1,0:T(4,128)S(1)}, f32[1,4,1024]{2,1,0:T(4,128)S(1)}, f32[1,4,1024,128]{3,2,1,0:T(8,128)})) conditional(s32[]{:T(128)} %bitcast.95, (f32[1,4,1024]{2,1,0:T(4,128)S(1)}, f32[1,4,1024]{2,1,0:T(4,128)S(1)}, f32[1,4,1024,128]{3,2,1,0:T(8,128)}) %tuple.69, (s32[1024]{0:T(1024)S(1)}, s32[1024]{0:T(1024)S(1)}, ...), branch_computations={%region_4.3_spmd, %region_5.6_spmd} | conditional | flops 2206216192 | bytes 77349464 | solution.py:71
  109.9 1.2 compare_and_fusion
  111.1 3.1 %fusion = (f32[4,1024]{1,0:T(4,128)S(1)}, f32[1024,1024,4]{1,0,2:T(8,128)S(1)}) fusion(pred[1024,1024]{0,1:T(8,128)(4,1)S(1)} %compare_and_fusion, bf16[1024,1,4,128]{3,0,2,1:T(8,128)(2,1)S(1)} %get-tuple-element.284, bf16[2048,1,128]{2,0,1:T(8,128)(2,1)S(1)} %get-tuple-element.282, s32[]{:T(128)} %get-tuple-element.283), kind=kOutput, calls=%fused_computation.2 | convolution fusion | flops 1086320640 | bytes 19152900 | tf_op jit(solution)/shard_map/while/body/eval_jaxpr/while/body/eval_jaxpr/cond/branch_1_fun/qhgd,khd->hgqk/dot_general | solution.py:51
  114.3 4.2 %fusion.2 = f32[4,1024]{1,0:T(4,128)S(1)} fusion(f32[1024,1024,4]{1,0,2:T(8,128)S(1)} %get-tuple-element.379, f32[4,1024]{1,0:T(4,128)S(1)} %bitcast.97, pred[1024,1024]{0,1:T(8,128)(4,1)S(1)} %compare_and_fusion), kind=kLoop, calls=%fused_computation.4 | loop fusion | flops 20967424 | bytes 17858560 | tf_op jit(solution)/shard_map/while/body/eval_jaxpr/while/body/eval_jaxpr/cond/branch_1_fun/reduce_sum | solution.py:58
  118.5 6.4 %bitcast_add_fusion = f32[1,4,1024,128]{3,2,1,0:T(8,128)S(1)} fusion(f32[1,4,1024,128]{3,2,1,0:T(8,128)S(1)} %copy-done.1, f32[1024,1024,4]{1,0,2:T(8,128)S(1)} %get-tuple-element.379, f32[4,1024]{1,0:T(4,128)S(1)} %bitcast.98, pred[1024,1024]{0,1:T(8,128)(4,1)S(1)} %compare_and_fusion, f32[4,1024]{1,0:T(4,128)S(1)} %get-tuple-element.376, ...), kind=kOutput, calls=%fused_computation.9 | convolution fusion | flops 1095761920 | bytes 22315520 | tf_op jit(solution)/shard_map/while/body/eval_jaxpr/while/body/eval_jaxpr/cond/branch_1_fun/hgqk,khd->hgqd/dot_general | solution.py:59
  124.9 1.3 copy-done.2
  132.0 16.3 %conditional.2 = ((f32[1,4,1024]{2,1,0:T(4,128)S(1)}, f32[1,4,1024]{2,1,0:T(4,128)S(1)}, f32[1,4,1024,128]{3,2,1,0:T(8,128)})) conditional(s32[]{:T(128)} %bitcast.95, (f32[1,4,1024]{2,1,0:T(4,128)S(1)}, f32[1,4,1024]{2,1,0:T(4,128)S(1)}, f32[1,4,1024,128]{3,2,1,0:T(8,128)}) %tuple.69, (s32[1024]{0:T(1024)S(1)}, s32[1024]{0:T(1024)S(1)}, ...), branch_computations={%region_4.3_spmd, %region_5.6_spmd} | conditional | flops 2206216192 | bytes 77349464 | solution.py:71
  132.0 1.2 compare_and_fusion
  133.2 3.1 %fusion = (f32[4,1024]{1,0:T(4,128)S(1)}, f32[1024,1024,4]{1,0,2:T(8,128)S(1)}) fusion(pred[1024,1024]{0,1:T(8,128)(4,1)S(1)} %compare_and_fusion, bf16[1024,1,4,128]{3,0,2,1:T(8,128)(2,1)S(1)} %get-tuple-element.284, bf16[2048,1,128]{2,0,1:T(8,128)(2,1)S(1)} %get-tuple-element.282, s32[]{:T(128)} %get-tuple-element.283), kind=kOutput, calls=%fused_computation.2 | convolution fusion | flops 1086320640 | bytes 19152900 | tf_op jit(solution)/shard_map/while/body/eval_jaxpr/while/body/eval_jaxpr/cond/branch_1_fun/qhgd,khd->hgqk/dot_general | solution.py:51
  136.4 4.2 %fusion.2 = f32[4,1024]{1,0:T(4,128)S(1)} fusion(f32[1024,1024,4]{1,0,2:T(8,128)S(1)} %get-tuple-element.379, f32[4,1024]{1,0:T(4,128)S(1)} %bitcast.97, pred[1024,1024]{0,1:T(8,128)(4,1)S(1)} %compare_and_fusion), kind=kLoop, calls=%fused_computation.4 | loop fusion | flops 20967424 | bytes 17858560 | tf_op jit(solution)/shard_map/while/body/eval_jaxpr/while/body/eval_jaxpr/cond/branch_1_fun/reduce_sum | solution.py:58
  140.6 6.4 %bitcast_add_fusion = f32[1,4,1024,128]{3,2,1,0:T(8,128)S(1)} fusion(f32[1,4,1024,128]{3,2,1,0:T(8,128)S(1)} %copy-done.1, f32[1024,1024,4]{1,0,2:T(8,128)S(1)} %get-tuple-element.379, f32[4,1024]{1,0:T(4,128)S(1)} %bitcast.98, pred[1024,1024]{0,1:T(8,128)(4,1)S(1)} %compare_and_fusion, f32[4,1024]{1,0:T(4,128)S(1)} %get-tuple-element.376, ...), kind=kOutput, calls=%fused_computation.9 | convolution fusion | flops 1095761920 | bytes 22315520 | tf_op jit(solution)/shard_map/while/body/eval_jaxpr/while/body/eval_jaxpr/cond/branch_1_fun/hgqk,khd->hgqd/dot_general | solution.py:59
  147.0 1.3 copy-done.2
  148.3 2.0 %fusion.28 = bf16[1024,1,4,128]{3,0,2,1:T(8,128)(2,1)S(1)} fusion(f32[1,4,1024,128]{3,2,1,0:T(8,128)} %get-tuple-element.510, f32[4,1024]{1,0:T(4,128)S(1)} %bitcast.100), kind=kLoop, calls=%fused_computation.28.clone.1 | loop fusion | flops 1048576 | bytes 3162112 | tf_op jit(solution)/shard_map/while/body/eval_jaxpr/convert_element_type | solution.py:102
  150.3 0.8 copy.53
  151.6 1.0 constant_dynamic-update-slice_fusion.2
  152.6 30.1 %all_to_all.67 = bf16[8,256,512]{2,1,0:T(8,128)(2,1)S(1)} all-to-all(bf16[8,256,512]{2,1,0:T(8,128)(2,1)} %bitcast.105), channel_id=1, replica_groups=mesh['seq'=8,'grp'=4] {'seq'}, dimensions={0} | all-to-all | bytes 4194304 | tf_op jit(solution)/shard_map/all_to_all | solution.py:158
  182.7 2.4 %copy.37 = bf16[8,256,512]{1,2,0:T(8,128)(2,1)} copy(bf16[8,256,512]{2,1,0:T(8,128)(2,1)S(1)} %all_to_all.67) | data formatting | bytes 4194304 | tf_op jit(solution)/shard_map/all_to_all | solution.py:158
  185.1 4.1 %copy.38 = bf16[256,4096]{1,0:T(8,128)(2,1)} copy(bf16[256,4096]{0,1:T(8,128)(2,1)} %bitcast.103) | data formatting | bytes 4194304 | tf_op jit(solution)/shard_map/all_to_all | solution.py:158
  (59 shorter events, 9.0 us)
Async XLA Ops:
  0.0 1.0 copy-start
  1.9 14.9 %all-to-all-start.1 = ((bf16[256,8,128]{2,0,1:T(8,128)(2,1)}), bf16[256,8,128]{2,0,1:T(8,128)(2,1)S(1)}, u32[]{:S(2)}, u32[]{:S(2)}) async-start(bf16[256,8,128]{2,0,1:T(8,128)(2,1)} %copy_bitcast_fusion.3), calls=%async_computation.1 | async-start | bytes 1048576 | tf_op jit(solution)/shard_map/all_to_all | solution.py:128
  10.3 40.9 %copy-start.3 = (s32[6]{0:T(128)S(1)}, s32[6]{0:T(128)}, u32[]{:S(2)}) copy-start(s32[6]{0:T(128)} %param.13) | copy-start | bytes 76
  16.8 30.2 %all-to-all-start = ((bf16[256,8,512]{2,0,1:T(8,128)(2,1)}), bf16[256,8,512]{2,0,1:T(8,128)(2,1)S(1)}, u32[]{:S(2)}, u32[]{:S(2)}) async-start(bf16[256,8,512]{2,0,1:T(8,128)(2,1)} %bitcast.102), calls=%async_computation | async-start | bytes 4194304 | tf_op jit(solution)/shard_map/all_to_all | solution.py:127
  47.0 13.9 %all-to-all-start.2 = ((bf16[256,8,128]{2,0,1:T(8,128)(2,1)}), bf16[256,8,128]{2,0,1:T(8,128)(2,1)}, u32[]{:S(2)}, u32[]{:S(2)}) async-start(bf16[256,8,128]{2,0,1:T(8,128)(2,1)} %copy_bitcast_fusion.2), calls=%async_computation.2 | async-start | bytes 1048576 | tf_op jit(solution)/shard_map/all_to_all | solution.py:129
  76.9 4.2 %copy-start.1 = (f32[1,4,1024,128]{3,2,1,0:T(8,128)S(1)}, f32[1,4,1024,128]{3,2,1,0:T(8,128)}, u32[]{:S(2)}) copy-start(f32[1,4,1024,128]{3,2,1,0:T(8,128)} %get-tuple-element.286) | copy-start | bytes 6291460 | tf_op jit(solution)/shard_map/while/body/eval_jaxpr/while/body/eval_jaxpr/cond
  87.5 1.3 copy-start.2
  114.3 4.2 %copy-start.1 = (f32[1,4,1024,128]{3,2,1,0:T(8,128)S(1)}, f32[1,4,1024,128]{3,2,1,0:T(8,128)}, u32[]{:S(2)}) copy-start(f32[1,4,1024,128]{3,2,1,0:T(8,128)} %get-tuple-element.286) | copy-start | bytes 6291460 | tf_op jit(solution)/shard_map/while/body/eval_jaxpr/while/body/eval_jaxpr/cond
  124.9 1.3 copy-start.2
  136.4 4.2 %copy-start.1 = (f32[1,4,1024,128]{3,2,1,0:T(8,128)S(1)}, f32[1,4,1024,128]{3,2,1,0:T(8,128)}, u32[]{:S(2)}) copy-start(f32[1,4,1024,128]{3,2,1,0:T(8,128)} %get-tuple-element.286) | copy-start | bytes 6291460 | tf_op jit(solution)/shard_map/while/body/eval_jaxpr/while/body/eval_jaxpr/cond
  147.0 1.3 copy-start.2
where the time goes:
time: 190 us; the launch traced here: 189 us
  local copies, waits for them, and re-layouts  41.2 us (22%)
  waiting for transfers between devices  38.5 us (20%)
  blocking collectives  30.1 us (16%)
  matrix products  28.5 us (15%)
  other arithmetic  20.5 us (11%)
  loops' own time  17.4 us (9%)
  starting transfers between devices  13 us (7%)
    all_to_all x1, blocking collectives, on_device(): lax.all_to_all(outputs, 'seq', split_axis=0, concat_axis=1, tiled=True)  30.1 us
    all_to_all x1, waiting for transfers between devices, on_device(): lax.all_to_all(queries, 'seq', split_axis=1, concat_axis=0, tiled=True)  24.6 us
    dot_general x3, matrix products, compute(): jnp.einsum('hgqk,khd->hgqd', weights.astype(jnp.bfloat16), value_part, pr...  19.1 us
    another operation x2, loops' own time, sweep_keys(): return lax.fori_loop(0, turns, advance, running)  15.7 us
    reduce_sum x3, other arithmetic, compute(): totals = totals * rescale + jnp.sum(weights, axis=-1)  12.6 us
    dot_general x3, matrix products, compute(): jnp.einsum('qhgd,khd->hgqk', query_rows, key_part, preferred_element_type...  9.44 us
    all_to_all x1, waiting for transfers between devices, on_device(): lax.all_to_all(value_send, 'seq', split_axis=1, concat_axis=0, tiled=True)  7.32 us
    all_to_all x1, waiting for transfers between devices, on_device(): lax.all_to_all(key_send, 'seq', split_axis=1, concat_axis=0, tiled=True)  6.57 us
  transfers between devices with their start and end apart: 3, of which 3 were waited for; matrix products, arithmetic and copies ran while one was open for 4% of the time, Pallas kernels for 0%

commit v1 on v0

--- a/solution.py
+++ b/solution.py
@@ -1,11 +1,25 @@
+import functools
 import jax
 import jax.numpy as jnp
 from jax import lax
 from jax.sharding import PartitionSpec as P
+from jax.lax import all_to_all, axis_size
 
 HEAD_DIM = 128
 DOC_UNIT = 128
 lowest = -1e30
+
+
+def fix_the_ladders(arr_in, link_axis):
+    return jnp.concatenate(
+        all_to_all(
+            jnp.stack(jnp.split(arr_in, axis_size(link_axis), axis=1), axis=0), link_axis, 0, 0
+        ),
+        axis=0,
+    )
+
+
+enter_copies = functools.partial(fix_the_ladders, link_axis="seq")
 
 
 def doc_starts(doc_lengths):
@@ -125,7 +139,7 @@
     ).reshape(row_count, seq_count * kv_dev * head_dim)
     all_queries, all_keys, all_values = (
         lax.all_to_all(queries, "seq", split_axis=1, concat_axis=0, tiled=True),
-        lax.all_to_all(key_send, "seq", split_axis=1, concat_axis=0, tiled=True),
+        enter_copies(key_send),
         lax.all_to_all(value_send, "seq", split_axis=1, concat_axis=0, tiled=True),
     )
     total_rows = all_queries.shape[0]

time: 190 us -> 200 us (1.053)
  local copies, waits for them, and re-layouts: 41.2 us -> 50 us
    unnamed x4 -> x11, local copies, waits for them, and re-layouts: 1.05 us -> 10.4 us
    another operation x6 -> x7, local copies, waits for them, and re-layouts: 2.91 us -> 4.38 us
  transfers between devices with their start and end apart: 3 -> 3, of which waited for: 3 -> 3; matrix products, arithmetic and copies ran while one was open for 4% -> 3% of each run, Pallas kernels for 0% -> 0%
where the time goes in v1:
time: 200 us; the launch traced here: 199 us
  local copies, waits for them, and re-layouts  50 us (25%)
  waiting for transfers between devices  39.5 us (20%)
  blocking collectives  30.1 us (15%)
  matrix products  28.5 us (14%)
  other arithmetic  20.5 us (10%)
  loops' own time  17.4 us (9%)
  starting transfers between devices  13 us (6%)
    all_to_all x1, blocking collectives, on_device(): lax.all_to_all(outputs, 'seq', split_axis=0, concat_axis=1, tiled=True)  30.1 us
    all_to_all x1, waiting for transfers between devices, on_device(): lax.all_to_all(queries, 'seq', split_axis=1, concat_axis=0, tiled=True)  25.6 us
    dot_general x3, matrix products, compute(): jnp.einsum('hgqk,khd->hgqd', weights.astype(jnp.bfloat16), value_part, pr...  19.1 us
    another operation x2, loops' own time, sweep_keys(): return lax.fori_loop(0, turns, advance, running)  15.7 us
    reduce_sum x3, other arithmetic, compute(): totals = totals * rescale + jnp.sum(weights, axis=-1)  12.6 us
    unnamed x11, local copies, waits for them, and re-layouts  10.4 us
    dot_general x3, matrix products, compute(): jnp.einsum('qhgd,khd->hgqk', query_rows, key_part, preferred_element_type...  9.44 us
    all_to_all x1, waiting for transfers between devices, on_device(): lax.all_to_all(value_send, 'seq', split_axis=1, concat_axis=0, tiled=True)  7.32 us
  transfers between devices with their start and end apart: 3, of which 3 were waited for; matrix products, arithmetic and copies ran while one was open for 3% of the time, Pallas kernels for 0%

profile of v1, /device:TPU:0, one launch (start us, length us, event | category | flops | bytes accessed | tf_op | source)
XLA Modules:
  0.0 199.0 jit_solution(15180586394917760287)
XLA Ops:
  0.0 1.5 bitcast_dynamic-update-slice_fusion.7
  1.5 1.5 bitcast_dynamic-update-slice_fusion.6
  3.0 1.5 bitcast_dynamic-update-slice_fusion.5
  4.5 1.5 bitcast_dynamic-update-slice_fusion.4
  6.0 1.5 bitcast_dynamic-update-slice_fusion.3
  7.4 1.5 bitcast_dynamic-update-slice_fusion.2
  8.9 1.5 bitcast_dynamic-update-slice_fusion.1
  10.4 1.5 bitcast_dynamic-update-slice_fusion
  11.8 5.2 %all-to-all-start.1 = ((bf16[8,256,128]{2,1,0:T(8,128)(2,1)}), bf16[8,256,128]{2,1,0:T(8,128)(2,1)S(1)}, u32[]{:S(2)}, u32[]{:S(2)}) async-start(bf16[8,256,128]{2,1,0:T(8,128)(2,1)} %bitcast_dynamic-update-slice_fusion), calls=%async_computation.1 | async-start | bytes 1048576 | tf_op jit(solution)/shard_map/all_to_all | solution.py:15
  17.0 3.1 %copy.42 = bf16[32,8,8,512]{3,2,0,1:T(8,128)(2,1)} copy(bf16[32,8,8,512]{3,2,1,0:T(8,128)(2,1)} %bitcast.113) | data formatting | bytes 4194304 | tf_op jit(solution)/shard_map/all_to_all | solution.py:141
  20.2 6.6 %all-to-all-done.1 = bf16[8,256,128]{2,1,0:T(8,128)(2,1)S(1)} async-done(((bf16[8,256,128]{2,1,0:T(8,128)(2,1)}), bf16[8,256,128]{2,1,0:T(8,128)(2,1)S(1)}, u32[]{:S(2)}, u32[]{:S(2)}) %all-to-all-start.1) | async-done | bytes 524320 | tf_op jit(solution)/shard_map/all_to_all | solution.py:15
  26.8 3.6 %all-to-all-start = ((bf16[256,8,512]{2,0,1:T(8,128)(2,1)}), bf16[256,8,512]{2,0,1:T(8,128)(2,1)S(1)}, u32[]{:S(2)}, u32[]{:S(2)}) async-start(bf16[256,8,512]{2,0,1:T(8,128)(2,1)} %bitcast.111), calls=%async_computation | async-start | bytes 4194304 | tf_op jit(solution)/shard_map/all_to_all | solution.py:141
  31.3 25.6 %all-to-all-done = bf16[256,8,512]{2,0,1:T(8,128)(2,1)S(1)} async-done(((bf16[256,8,512]{2,0,1:T(8,128)(2,1)}), bf16[256,8,512]{2,0,1:T(8,128)(2,1)S(1)}, u32[]{:S(2)}, u32[]{:S(2)}) %all-to-all-start) | async-done | bytes 2097184 | tf_op jit(solution)/shard_map/all_to_all | solution.py:141
  56.9 4.1 %all-to-all-start.2 = ((bf16[256,8,128]{2,0,1:T(8,128)(2,1)}), bf16[256,8,128]{2,0,1:T(8,128)(2,1)}, u32[]{:S(2)}, u32[]{:S(2)}) async-start(bf16[256,8,128]{2,0,1:T(8,128)(2,1)} %copy_bitcast_fusion.2), calls=%async_computation.2 | async-start | bytes 1048576 | tf_op jit(solution)/shard_map/all_to_all | solution.py:143
  61.4 2.1 %reshape.174 = bf16[2,1024,1,4,128]{4,3,1,0,2:T(4,128)(2,1)} reshape(bf16[8,256,512]{2,1,0:T(8,128)(2,1)S(1)} %bitcast.110) | data formatting | bytes 4194304 | tf_op jit(solution)/shard_map/reshape | solution.py:150
  63.5 7.3 %all-to-all-done.2 = bf16[256,8,128]{2,0,1:T(8,128)(2,1)} async-done(((bf16[256,8,128]{2,0,1:T(8,128)(2,1)}), bf16[256,8,128]{2,0,1:T(8,128)(2,1)}, u32[]{:S(2)}, u32[]{:S(2)}) %all-to-all-start.2) | async-done | bytes 524320 | tf_op jit(solution)/shard_map/all_to_all | solution.py:143
  71.4 91.1 %while.28 = (s32[]{:T(128)}, bf16[2,1024,512]{2,1,0:T(8,128)(2,1)}, s32[2]{0:T(128)}, s32[2048]{0:T(1024)S(1)}, bf16[2,1024,1,4,128]{4,3,1,0,2:T(4,128)(2,1)}, /...) while((s32[]{:T(128)}, bf16[2,1024,512]{2,1,0:T(8,128)(2,1)}, ...), condition=%wide.region_9.10_spmd, body=%wide.region_2.9_spmd.sunk | while | flops 2207266816 | bytes 93153088 | solution.py:170
  71.4 1.3 dynamic_slice.58
  73.4 1.6 constant_dynamic-slice_fusion.2
  75.2 1.4 broadcast.86
  76.6 27.9 %while.29 = (s32[]{:T(128)}, f32[1,4,1024]{2,1,0:T(4,128)S(1)}, f32[1,4,1024]{2,1,0:T(4,128)S(1)}, f32[1,4,1024,128]{3,2,1,0:T(8,128)}, s32[1024]{0:T(1024)S(1)}...) while((s32[]{:T(128)}, f32[1,4,1024]{2,1,0:T(4,128)S(1)}, ...), condition=%wide.region_8.8_spmd, body=%wide.region_3.7_spmd.sunk | while | flops 2206217216 | bytes 77362136 | solution.py:106
  82.4 16.3 %conditional.2 = ((f32[1,4,1024]{2,1,0:T(4,128)S(1)}, f32[1,4,1024]{2,1,0:T(4,128)S(1)}, f32[1,4,1024,128]{3,2,1,0:T(8,128)})) conditional(s32[]{:T(128)} %bitcast.104, (f32[1,4,1024]{2,1,0:T(4,128)S(1)}, f32[1,4,1024]{2,1,0:T(4,128)S(1)}, f32[1,4,1024,128]{3,2,1,0:T(8,128)}) %tuple.69, (s32[1024]{0:T(1024)S(1)}, s32[1024]{0:T(1024)S(1)}, ...), branch_computations={%region_4.3_spmd, %region_5.6_spmd} | conditional | flops 2206216192 | bytes 77349464 | solution.py:85
  82.4 1.2 compare_and_fusion
  83.6 3.1 %fusion = (f32[4,1024]{1,0:T(4,128)S(1)}, f32[1024,1024,4]{1,0,2:T(8,128)S(1)}) fusion(pred[1024,1024]{0,1:T(8,128)(4,1)S(1)} %compare_and_fusion, bf16[1024,1,4,128]{3,0,2,1:T(8,128)(2,1)S(1)} %get-tuple-element.284, bf16[2048,1,128]{2,0,1:T(8,128)(2,1)S(1)} %get-tuple-element.282, s32[]{:T(128)} %get-tuple-element.283), kind=kOutput, calls=%fused_computation.2 | convolution fusion | flops 1086320640 | bytes 19152900 | tf_op jit(solution)/shard_map/while/body/eval_jaxpr/while/body/eval_jaxpr/cond/branch_1_fun/qhgd,khd->hgqk/dot_general | solution.py:65
  86.8 4.2 %fusion.2 = f32[4,1024]{1,0:T(4,128)S(1)} fusion(f32[1024,1024,4]{1,0,2:T(8,128)S(1)} %get-tuple-element.379, f32[4,1024]{1,0:T(4,128)S(1)} %bitcast.106, pred[1024,1024]{0,1:T(8,128)(4,1)S(1)} %compare_and_fusion), kind=kLoop, calls=%fused_computation.4 | loop fusion | flops 20967424 | bytes 17858560 | tf_op jit(solution)/shard_map/while/body/eval_jaxpr/while/body/eval_jaxpr/cond/branch_1_fun/reduce_sum | solution.py:72
  91.0 6.4 %bitcast_add_fusion = f32[1,4,1024,128]{3,2,1,0:T(8,128)S(1)} fusion(f32[1,4,1024,128]{3,2,1,0:T(8,128)S(1)} %copy-done.1, f32[1024,1024,4]{1,0,2:T(8,128)S(1)} %get-tuple-element.379, f32[4,1024]{1,0:T(4,128)S(1)} %bitcast.107, pred[1024,1024]{0,1:T(8,128)(4,1)S(1)} %compare_and_fusion, f32[4,1024]{1,0:T(4,128)S(1)} %get-tuple-element.376, ...), kind=kOutput, calls=%fused_computation.9 | convolution fusion | flops 1095761920 | bytes 22315520 | tf_op jit(solution)/shard_map/while/body/eval_jaxpr/while/body/eval_jaxpr/cond/branch_1_fun/hgqk,khd->hgqd/dot_general | solution.py:73
  97.4 1.3 copy-done.2
  104.5 2.0 fusion.27
  108.8 1.3 dynamic_slice.58
  110.8 1.6 constant_dynamic-slice_fusion.2
  112.6 1.4 broadcast.86
  114.0 44.2 %while.29 = (s32[]{:T(128)}, f32[1,4,1024]{2,1,0:T(4,128)S(1)}, f32[1,4,1024]{2,1,0:T(4,128)S(1)}, f32[1,4,1024,128]{3,2,1,0:T(8,128)}, s32[1024]{0:T(1024)S(1)}...) while((s32[]{:T(128)}, f32[1,4,1024]{2,1,0:T(4,128)S(1)}, ...), condition=%wide.region_8.8_spmd, body=%wide.region_3.7_spmd.sunk | while | flops 2206217216 | bytes 77362136 | solution.py:106
  119.8 16.3 %conditional.2 = ((f32[1,4,1024]{2,1,0:T(4,128)S(1)}, f32[1,4,1024]{2,1,0:T(4,128)S(1)}, f32[1,4,1024,128]{3,2,1,0:T(8,128)})) conditional(s32[]{:T(128)} %bitcast.104, (f32[1,4,1024]{2,1,0:T(4,128)S(1)}, f32[1,4,1024]{2,1,0:T(4,128)S(1)}, f32[1,4,1024,128]{3,2,1,0:T(8,128)}) %tuple.69, (s32[1024]{0:T(1024)S(1)}, s32[1024]{0:T(1024)S(1)}, ...), branch_computations={%region_4.3_spmd, %region_5.6_spmd} | conditional | flops 2206216192 | bytes 77349464 | solution.py:85
  119.8 1.2 compare_and_fusion
  121.0 3.1 %fusion = (f32[4,1024]{1,0:T(4,128)S(1)}, f32[1024,1024,4]{1,0,2:T(8,128)S(1)}) fusion(pred[1024,1024]{0,1:T(8,128)(4,1)S(1)} %compare_and_fusion, bf16[1024,1,4,128]{3,0,2,1:T(8,128)(2,1)S(1)} %get-tuple-element.284, bf16[2048,1,128]{2,0,1:T(8,128)(2,1)S(1)} %get-tuple-element.282, s32[]{:T(128)} %get-tuple-element.283), kind=kOutput, calls=%fused_computation.2 | convolution fusion | flops 1086320640 | bytes 19152900 | tf_op jit(solution)/shard_map/while/body/eval_jaxpr/while/body/eval_jaxpr/cond/branch_1_fun/qhgd,khd->hgqk/dot_general | solution.py:65
  124.2 4.2 %fusion.2 = f32[4,1024]{1,0:T(4,128)S(1)} fusion(f32[1024,1024,4]{1,0,2:T(8,128)S(1)} %get-tuple-element.379, f32[4,1024]{1,0:T(4,128)S(1)} %bitcast.106, pred[1024,1024]{0,1:T(8,128)(4,1)S(1)} %compare_and_fusion), kind=kLoop, calls=%fused_computation.4 | loop fusion | flops 20967424 | bytes 17858560 | tf_op jit(solution)/shard_map/while/body/eval_jaxpr/while/body/eval_jaxpr/cond/branch_1_fun/reduce_sum | solution.py:72
  128.5 6.4 %bitcast_add_fusion = f32[1,4,1024,128]{3,2,1,0:T(8,128)S(1)} fusion(f32[1,4,1024,128]{3,2,1,0:T(8,128)S(1)} %copy-done.1, f32[1024,1024,4]{1,0,2:T(8,128)S(1)} %get-tuple-element.379, f32[4,1024]{1,0:T(4,128)S(1)} %bitcast.107, pred[1024,1024]{0,1:T(8,128)(4,1)S(1)} %compare_and_fusion, f32[4,1024]{1,0:T(4,128)S(1)} %get-tuple-element.376, ...), kind=kOutput, calls=%fused_computation.9 | convolution fusion | flops 1095761920 | bytes 22315520 | tf_op jit(solution)/shard_map/while/body/eval_jaxpr/while/body/eval_jaxpr/cond/branch_1_fun/hgqk,khd->hgqd/dot_general | solution.py:73
  134.8 1.3 copy-done.2
  141.9 16.3 %conditional.2 = ((f32[1,4,1024]{2,1,0:T(4,128)S(1)}, f32[1,4,1024]{2,1,0:T(4,128)S(1)}, f32[1,4,1024,128]{3,2,1,0:T(8,128)})) conditional(s32[]{:T(128)} %bitcast.104, (f32[1,4,1024]{2,1,0:T(4,128)S(1)}, f32[1,4,1024]{2,1,0:T(4,128)S(1)}, f32[1,4,1024,128]{3,2,1,0:T(8,128)}) %tuple.69, (s32[1024]{0:T(1024)S(1)}, s32[1024]{0:T(1024)S(1)}, ...), branch_computations={%region_4.3_spmd, %region_5.6_spmd} | conditional | flops 2206216192 | bytes 77349464 | solution.py:85
  141.9 1.2 compare_and_fusion
  143.1 3.1 %fusion = (f32[4,1024]{1,0:T(4,128)S(1)}, f32[1024,1024,4]{1,0,2:T(8,128)S(1)}) fusion(pred[1024,1024]{0,1:T(8,128)(4,1)S(1)} %compare_and_fusion, bf16[1024,1,4,128]{3,0,2,1:T(8,128)(2,1)S(1)} %get-tuple-element.284, bf16[2048,1,128]{2,0,1:T(8,128)(2,1)S(1)} %get-tuple-element.282, s32[]{:T(128)} %get-tuple-element.283), kind=kOutput, calls=%fused_computation.2 | convolution fusion | flops 1086320640 | bytes 19152900 | tf_op jit(solution)/shard_map/while/body/eval_jaxpr/while/body/eval_jaxpr/cond/branch_1_fun/qhgd,khd->hgqk/dot_general | solution.py:65
  146.3 4.2 %fusion.2 = f32[4,1024]{1,0:T(4,128)S(1)} fusion(f32[1024,1024,4]{1,0,2:T(8,128)S(1)} %get-tuple-element.379, f32[4,1024]{1,0:T(4,128)S(1)} %bitcast.106, pred[1024,1024]{0,1:T(8,128)(4,1)S(1)} %compare_and_fusion), kind=kLoop, calls=%fused_computation.4 | loop fusion | flops 20967424 | bytes 17858560 | tf_op jit(solution)/shard_map/while/body/eval_jaxpr/while/body/eval_jaxpr/cond/branch_1_fun/reduce_sum | solution.py:72
  150.5 6.4 %bitcast_add_fusion = f32[1,4,1024,128]{3,2,1,0:T(8,128)S(1)} fusion(f32[1,4,1024,128]{3,2,1,0:T(8,128)S(1)} %copy-done.1, f32[1024,1024,4]{1,0,2:T(8,128)S(1)} %get-tuple-element.379, f32[4,1024]{1,0:T(4,128)S(1)} %bitcast.107, pred[1024,1024]{0,1:T(8,128)(4,1)S(1)} %compare_and_fusion, f32[4,1024]{1,0:T(4,128)S(1)} %get-tuple-element.376, ...), kind=kOutput, calls=%fused_computation.9 | convolution fusion | flops 1095761920 | bytes 22315520 | tf_op jit(solution)/shard_map/while/body/eval_jaxpr/while/body/eval_jaxpr/cond/branch_1_fun/hgqk,khd->hgqd/dot_general | solution.py:73
  156.9 1.3 copy-done.2
  158.2 2.0 fusion.27
  162.5 30.1 %all_to_all.56 = bf16[8,256,512]{2,1,0:T(8,128)(2,1)S(1)} all-to-all(bf16[8,256,512]{2,1,0:T(8,128)(2,1)} %bitcast.114), channel_id=1, replica_groups=mesh['seq'=8,'grp'=4] {'seq'}, dimensions={0} | all-to-all | bytes 4194304 | tf_op jit(solution)/shard_map/all_to_all | solution.py:172
  192.6 2.4 %copy.32 = bf16[8,256,512]{1,2,0:T(8,128)(2,1)} copy(bf16[8,256,512]{2,1,0:T(8,128)(2,1)S(1)} %all_to_all.56) | data formatting | bytes 4194304 | tf_op jit(solution)/shard_map/all_to_all | solution.py:172
  195.0 4.1 %copy.33 = bf16[256,4096]{1,0:T(8,128)(2,1)} copy(bf16[256,4096]{0,1:T(8,128)(2,1)} %bitcast.112) | data formatting | bytes 4194304 | tf_op jit(solution)/shard_map/all_to_all | solution.py:172
  (66 shorter events, 14.3 us)
Async XLA Ops:
  0.0 30.4 %copy-start = (bf16[256,1024]{1,0:T(8,128)(2,1)S(1)}, bf16[256,1024]{1,0:T(8,128)(2,1)}, u32[]{:S(2)}) copy-start(bf16[256,1024]{1,0:T(8,128)(2,1)} %param.12) | copy-start | bytes 1572868
  11.8 14.9 %all-to-all-start.1 = ((bf16[8,256,128]{2,1,0:T(8,128)(2,1)}), bf16[8,256,128]{2,1,0:T(8,128)(2,1)S(1)}, u32[]{:S(2)}, u32[]{:S(2)}) async-start(bf16[8,256,128]{2,1,0:T(8,128)(2,1)} %bitcast_dynamic-update-slice_fusion), calls=%async_computation.1 | async-start | bytes 1048576 | tf_op jit(solution)/shard_map/all_to_all | solution.py:15
  20.2 40.9 %copy-start.3 = (s32[6]{0:T(128)S(1)}, s32[6]{0:T(128)}, u32[]{:S(2)}) copy-start(s32[6]{0:T(128)} %param.13) | copy-start | bytes 76
  26.8 30.2 %all-to-all-start = ((bf16[256,8,512]{2,0,1:T(8,128)(2,1)}), bf16[256,8,512]{2,0,1:T(8,128)(2,1)S(1)}, u32[]{:S(2)}, u32[]{:S(2)}) async-start(bf16[256,8,512]{2,0,1:T(8,128)(2,1)} %bitcast.111), calls=%async_computation | async-start | bytes 4194304 | tf_op jit(solution)/shard_map/all_to_all | solution.py:141
  56.9 13.9 %all-to-all-start.2 = ((bf16[256,8,128]{2,0,1:T(8,128)(2,1)}), bf16[256,8,128]{2,0,1:T(8,128)(2,1)}, u32[]{:S(2)}, u32[]{:S(2)}) async-start(bf16[256,8,128]{2,0,1:T(8,128)(2,1)} %copy_bitcast_fusion.2), calls=%async_computation.2 | async-start | bytes 1048576 | tf_op jit(solution)/shard_map/all_to_all | solution.py:143
  86.8 4.2 %copy-start.1 = (f32[1,4,1024,128]{3,2,1,0:T(8,128)S(1)}, f32[1,4,1024,128]{3,2,1,0:T(8,128)}, u32[]{:S(2)}) copy-start(f32[1,4,1024,128]{3,2,1,0:T(8,128)} %get-tuple-element.286) | copy-start | bytes 6291460 | tf_op jit(solution)/shard_map/while/body/eval_jaxpr/while/body/eval_jaxpr/cond
  97.4 1.3 copy-start.2
  124.2 4.2 %copy-start.1 = (f32[1,4,1024,128]{3,2,1,0:T(8,128)S(1)}, f32[1,4,1024,128]{3,2,1,0:T(8,128)}, u32[]{:S(2)}) copy-start(f32[1,4,1024,128]{3,2,1,0:T(8,128)} %get-tuple-element.286) | copy-start | bytes 6291460 | tf_op jit(solution)/shard_map/while/body/eval_jaxpr/while/body/eval_jaxpr/cond
  134.8 1.3 copy-start.2
  146.3 4.2 %copy-start.1 = (f32[1,4,1024,128]{3,2,1,0:T(8,128)S(1)}, f32[1,4,1024,128]{3,2,1,0:T(8,128)}, u32[]{:S(2)}) copy-start(f32[1,4,1024,128]{3,2,1,0:T(8,128)} %get-tuple-element.286) | copy-start | bytes 6291460 | tf_op jit(solution)/shard_map/while/body/eval_jaxpr/while/body/eval_jaxpr/cond
  156.9 1.3 copy-start.2
